TPU v7x, 512 devices: a whole 4x4x16 slice. The times are simulated.
512 devices in a mesh: exp: 64 (over x, z), rep: 8 (over y, core).
Axes of the slice: x: 4, y: 4, z: 16, core: 2. Of those that a mesh axis runs over, the one named last changes fastest.
Arguments:
- latent: bfloat16 [128, 16, 64], P('exp'), may hold values from -6 to 6
- stem_weight: bfloat16 [144, 1536], replicated, may hold values from -0.5 to 0.5
- norm_gain: float32 [1536], replicated, may hold values from 0.4 to 1.6
- router_weight: bfloat16 [1536, 8], replicated, may hold values from -0.15625 to 0.15625
- routes: int32 [8192, 2], P('exp'), may hold values from 0 to 7, all different within a row; in each aligned block of 128 rows (0 to 127, 128 to 255, ...) at most 40 rows name the same one
- gate_weight: bfloat16 [1536, 24576], P('rep', 'exp'), may hold values from -0.15625 to 0.15625
- up_weight: bfloat16 [1536, 24576], P('rep', 'exp'), may hold values from -0.15625 to 0.15625
- down_weight: bfloat16 [24576, 1536], P('exp', 'rep'), may hold values from -0.109375 to 0.109375
- grad_mixed: bfloat16 [8192, 1536], P('exp'), may hold values from -6 to 6
Outputs:
- mixed: bfloat16 [8192, 1536], P('exp')
- grad_latent: float32 [128, 16, 64], P('exp')
- grad_gate: float32 [1536, 24576], P('rep', 'exp')
- grad_up: float32 [1536, 24576], P('rep', 'exp')
- grad_down: float32 [24576, 1536], P('exp', 'rep')
Inputs may be any that keep to these rules, and one draw needn't show every extreme that they name: `routes`: A token's 2 experts differ. Within the 128 tokens of one device, no expert is named more than 40 times, and in every draw some device's tokens name some expert exactly 40 times.
All inputs are finite; a program needn't handle non-finite values.
Results may differ from a plain program's by a relative error of at most 0.023.
Values may be sent and summed in bfloat16 or wider, within the bound.
A program may use at most 64 MiB of HBM per device.

v0:
```python
import jax
import jax.numpy as jnp
from jax import lax
from jax.sharding import PartitionSpec as P

CAP = 40
F32 = jnp.float32
BF = jnp.bfloat16


def dot32(a, b, dims=None):
    if dims is None:
        return jnp.dot(a, b, preferred_element_type=F32)
    return lax.dot_general(a, b, (dims, ((), ())), preferred_element_type=F32)


def split(v):
    hi = v.astype(BF)
    return (hi, (v - hi.astype(F32)).astype(BF))


def halo(cells):
    count = lax.axis_size("exp")
    head, tail = (cells[:1], cells[-1:])
    return jnp.concatenate(
        [
            lax.ppermute(tail, "exp", [(i, i + 1) for i in range(count - 1)]),
            cells,
            lax.ppermute(head, "exp", [(i + 1, i) for i in range(count - 1)]),
        ],
        axis=0,
    )


def gating(picked):
    chosen = jax.nn.sigmoid(picked)
    return chosen / jnp.sum(chosen, axis=-1, keepdims=True)


def local(
    latent,
    stem_weight,
    norm_gain,
    router_weight,
    routes,
    gate_weight,
    up_weight,
    down_weight,
    grad_mixed,
):
    rows_here, channels, width = latent.shape
    taps, model_width = stem_weight.shape
    experts = router_weight.shape[1]
    top = routes.shape[1]
    tok = rows_here * width
    nrep = lax.axis_size("rep")
    nexp = lax.axis_size("exp")
    shards = nexp // experts
    sub = CAP // nrep
    rep = lax.axis_index("rep")
    across = [[e * shards + m for e in range(experts)] for m in range(shards)]
    along = [[e * shards + m for m in range(shards)] for e in range(experts)]
    dsl = model_width // nrep
    s_here = lax.dynamic_slice_in_dim(stem_weight, rep * dsl, dsl, 1)
    gain_here = lax.dynamic_slice_in_dim(norm_gain, rep * dsl, dsl, 0)
    sg_hi, sg_lo = split(s_here.astype(F32) * gain_here)
    w2 = jnp.concatenate([gate_weight, up_weight], axis=1)
    g_full = lax.psum(dot32(sg_hi, w2) + dot32(sg_lo, w2), "rep")
    g_hi, g_lo = split(g_full)
    down = lax.all_gather(down_weight, "rep", axis=1, tiled=True)
    padded = jnp.pad(halo(latent), ((0, 0), (0, 0), (1, 1)))
    pieces = jnp.stack(
        [padded[i : i + rows_here, :, j : j + width] for i in range(3) for j in range(3)], axis=0
    )
    patches = jnp.transpose(pieces, (1, 3, 0, 2)).reshape(tok, taps)
    stem = dot32(patches, stem_weight).astype(BF)
    sv = stem.astype(F32)
    rstd = lax.rsqrt(jnp.mean(sv * sv, axis=-1, keepdims=True) + 1e-06)
    normed = (sv * rstd * norm_gain).astype(BF)
    logits = dot32(normed, router_weight)
    selector = (routes[:, :, None] == jnp.arange(experts, dtype=jnp.int32)).astype(F32)
    picked = jnp.sum(logits[:, None, :] * selector, axis=-1)
    gates = gating(picked)
    sel_i = selector.astype(jnp.int32)
    both = jnp.sum(sel_i, axis=1)
    before = jnp.cumsum(both, axis=0) - both
    position = jnp.sum(sel_i * before[:, None, :], axis=-1)
    slot = routes * CAP + position
    slot_ids = jnp.arange(experts * CAP, dtype=jnp.int32)
    hot = [slot[:, k][:, None] == slot_ids[None, :] for k in range(top)]
    hot_here = [
        lax.dynamic_slice_in_dim(h.reshape(tok, experts, CAP), rep * sub, sub, 2).reshape(
            tok, experts * sub
        )
        for h in hot
    ]
    hot_any = sum((h.astype(BF) for h in hot_here))
    rstd_parts = split(rstd)
    gate_parts = [split(gates[:, k][:, None]) for k in range(top)]
    wide = jnp.concatenate(
        [grad_mixed, patches, rstd_parts[0], rstd_parts[1], jnp.zeros((tok, 110), BF)], axis=1
    )
    send = dot32(hot_any, wide, ((0,), (0,))).astype(BF)
    send_gate = sum(
        (
            dot32(hot_here[k].astype(BF), jnp.concatenate(gate_parts[k], axis=1), ((0,), (0,)))
            for k in range(top)
        )
    ).astype(BF)
    send = jnp.concatenate(
        [send[:, : model_width + 146], send_gate, send[:, model_width + 148 :]], axis=1
    )
    send = send.reshape(experts, sub, -1)
    stage = lax.all_to_all(
        send, "exp", split_axis=0, concat_axis=0, tiled=True, axis_index_groups=across
    )
    recv = lax.all_gather(stage, "exp", axis=0, tiled=True, axis_index_groups=along)
    flat = recv.reshape(-1, recv.shape[-1])
    gm = flat[:, :model_width]
    pr = flat[:, model_width : model_width + taps]
    extra = flat[:, model_width + taps : model_width + taps + 4].astype(F32)
    rs = extra[:, 0:1] + extra[:, 1:2]
    gt = extra[:, 2:3] + extra[:, 3:4]
    hid = gate_weight.shape[1]
    pre = rs * (dot32(pr, g_hi) + dot32(pr, g_lo))
    pg, pu = (pre[:, :hid], pre[:, hid:])
    sigma = jax.nn.sigmoid(pg)
    hidden = pg * sigma * pu
    hg = (gt * hidden).astype(BF)
    out = dot32(hg, down)
    u = dot32(gm, down, ((1,), (1,)))
    gg = jnp.sum(hidden * u, axis=-1, keepdims=True)
    gu = rs * gt * u
    dpre = jnp.concatenate(
        [gu * pu * sigma * (1.0 + pg * (1.0 - sigma)), gu * pg * sigma], axis=1
    ).astype(BF)
    back = dot32(dpre, g_hi, ((1,), (1,))) + dot32(dpre, g_lo, ((1,), (1,)))
    t_part = dot32(pr, dpre, ((0,), (0,)))
    d_part = dot32(gm, hg, ((0,), (0,)))
    gg_hi, gg_lo = split(gg)
    ret = jnp.concatenate(
        [out.astype(BF), back.astype(BF), gg_hi, gg_lo, jnp.zeros((out.shape[0], 110), BF)], axis=1
    ).reshape(shards, experts, sub, -1)
    summed = lax.psum_scatter(ret, "exp", scatter_dimension=0, axis_index_groups=along, tiled=True)[
        0
    ]
    mine = lax.all_to_all(
        summed, "exp", split_axis=0, concat_axis=0, tiled=True, axis_index_groups=across
    )
    slots_back = lax.all_gather(mine, "rep", axis=1, tiled=True).reshape(experts * CAP, -1)
    t_full = lax.psum(t_part, "rep")
    t_hi, t_lo = split(t_full)
    gw = (dot32(s_here, t_hi, ((0,), (0,))) + dot32(s_here, t_lo, ((0,), (0,)))) * gain_here[
        :, None
    ]
    grad_gate, grad_up = (gw[:, :hid], gw[:, hid:])
    grad_down = (
        lax.psum_scatter(d_part.astype(BF), "rep", scatter_dimension=0, tiled=True).astype(F32).T
    )
    hot_sum = sum((h.astype(BF) for h in hot))
    tok_sum = dot32(hot_sum, slots_back)
    mixed = (sv + tok_sum[:, :model_width]).astype(BF)
    ggs = slots_back[:, model_width + taps : model_width + taps + 2]
    grad_gates = jnp.concatenate(
        [jnp.sum(dot32(hot[k].astype(BF), ggs), axis=-1, keepdims=True) for k in range(top)], axis=1
    )
    _, gate_pull = jax.vjp(gating, picked)
    grad_picked = gate_pull(grad_gates)[0]
    grad_logits = jnp.sum(selector * grad_picked[:, :, None], axis=1)
    sg_all = stem_weight.astype(F32) * norm_gain
    rproj = jnp.dot(sg_all, router_weight.astype(F32), precision=lax.Precision.HIGHEST)
    b = tok_sum[:, model_width : model_width + taps] + rstd * jnp.dot(
        grad_logits, rproj.T, precision=lax.Precision.HIGHEST
    )
    c = jnp.sum(patches.astype(F32) * b, axis=-1, keepdims=True) * (rstd * rstd / model_width)
    proj = (
        dot32(grad_mixed, stem_weight, ((1,), (1,)))
        + b
        - c * dot32(stem, stem_weight, ((1,), (1,)))
    )
    block = halo(proj.reshape(rows_here, width, taps)).reshape(rows_here + 2, width, 9, channels)
    shifted = jnp.pad(block, ((0, 0), (1, 1), (0, 0), (0, 0)))
    terms = [
        shifted[2 - i : 2 - i + rows_here, 2 - j : 2 - j + width, 3 * i + j, :]
        for i in range(3)
        for j in range(3)
    ]
    grad_latent = sum(terms).transpose(0, 2, 1)
    return (mixed, grad_latent, grad_gate, grad_up, grad_down)


def solution(mesh):
    return jax.shard_map(
        local,
        mesh=mesh,
        in_specs=(
            P("exp", None, None),
            P(),
            P(),
            P(),
            P("exp", None),
            P("rep", "exp"),
            P("rep", "exp"),
            P("exp", "rep"),
            P("exp", None),
        ),
        out_specs=(
            P("exp", None),
            P("exp", None, None),
            P("rep", "exp"),
            P("rep", "exp"),
            P("exp", "rep"),
        ),
        check_vma=False,
    )
```

profile of v0, /device:TPU:96, one launch (start us, length us, event | category | flops | bytes accessed | tf_op | source)
XLA Modules:
  0.0 310.6 jit_solution(7389787148921936075)
XLA Ops:
  8.1 0.8 fusion.85
  8.8 5.0 %collective-permute-start = (bf16[1,16,64]{2,1,0:T(8,128)(2,1)S(1)}, bf16[1,16,64]{2,1,0:T(8,128)(2,1)S(1)}, u32[]{:S(2)}, u32[]{:S(2)}) collective-permute-start(bf16[1,16,64]{2,1,0:T(8,128)(2,1)S(1)} %get-tuple-element.47), channel_id=1, source_target_pairs={{0,8},{8,16},{16,24},{24,32},{32,40},{40,48},{48,56},{56,64},{64,7... | collective-permute-start | bytes 6152 | tf_op jit(solution)/shard_map/ppermute | solution.py:27
  13.9 1.9 collective-permute-start.1
  15.8 0.7 convert_reduce_fusion
  16.9 0.7 multiply_reduce_fusion.3
  17.6 0.7 multiply_add_fusion.1
  18.5 2.1 collective-permute-done.1
  20.6 0.8 fusion.59
  21.4 0.8 constant_dynamic-update-slice_fusion.7
  22.2 0.7 constant_dynamic-update-slice_fusion.4
  23.0 0.7 constant_dynamic-update-slice_fusion.1
  26.1 31.8 %all_to_all.10 = bf16[8,5,1792]{2,1,0:T(8,128)(2,1)S(1)} all-to-all(bf16[8,5,1792]{2,1,0:T(8,128)(2,1)S(1)} %reshape.239), channel_id=1, replica_groups={{0,64,128,192,256,320,384,448},{8,72,136,200,264,328,392,456},{16,80,14..., dimensions={0} | all-to-all | bytes 286720 | tf_op jit(solution)/shard_map/all_to_all | solution.py:114
  57.9 0.7 copy.149
  59.1 1.1 convolution_add_fusion.2
  60.2 0.7 all-gather.6.cloned.1.call-update
  61.0 46.7 %all-gather.4.cloned.1.call-done = bf16[64,5,1792]{2,0,1:T(8,128)(2,1)} async-done(((bf16[8,5,1792]{2,0,1:T(8,128)(2,1)}), bf16[64,5,1792]{2,0,1:T(8,128)(2,1)}) %all-gather.4.cloned.1.call-update) | async-done | bytes 1146896 | tf_op jit(solution)/shard_map/all_gather | solution.py:117
  107.7 1.9 copy.150
  109.6 1.3 reshape.240
  110.9 1.0 slice_convert_fusion
  112.3 23.1 %all-reduce.5.cloned.1.call-done = f32[144,768]{1,0:T(8,128)} async-done(((f32[144,768]{1,0:T(8,128)}), f32[144,768]{1,0:T(8,128)}) %all-reduce.5.cloned.1.call-update) | async-done | bytes 442384 | tf_op jit(solution)/shard_map/psum | solution.py:68
  135.4 1.4 fusion.29
  136.9 1.2 fusion
  138.1 11.5 %all-gather.6.cloned.1.call-done = bf16[384,1536]{0,1:T(8,128)(2,1)} async-done(((bf16[384,192]{0,1:T(8,128)(2,1)}), bf16[384,1536]{0,1:T(8,128)(2,1)}) %all-gather.6.cloned.1.call-update) | async-done | bytes 1179664 | tf_op jit(solution)/shard_map/all_gather | solution.py:70
  149.6 3.2 %multiply_convert_fusion.1 = (bf16[320,384]{1,0:T(8,128)(2,1)S(1)}, bf16[320,384]{1,0:T(8,128)(2,1)S(1)}, f32[320]{0:T(512)S(1)}, f32[320,384]{1,0:T(8,128)}) fusion(f32[320,768]{1,0:T(8,128)} %fusion, f32[320]{0:T(512)S(1)} %get-tuple-element.30, bf16[384,1536]{0,1:T(8,128)(2,1)} %all-gather.6.cloned.1.call-done, bf16[320,1792]{1,0:T(8,128)(2,1)S(1)} %copy-done.3), kind=kOutput, calls=%fused_computation.36 | convolution fusion | flops 379698880 | bytes 4132096 | tf_op jit(solution)/shard_map/dot_general | solution.py:14
  153.0 1.0 copy.155
  154.0 1.0 copy.154
  155.8 0.8 concatenate.73
  156.6 2.0 convolution_convert_fusion.1
  159.1 3.5 %concatenate.74 = bf16[8,8,5,1792]{3,2,1,0:T(8,128)(2,1)} concatenate(bf16[8,8,5,1536]{3,2,1,0:T(8,128)(2,1)S(1)} %concatenate.71, bf16[8,8,5,144]{3,2,1,0:T(8,128)(2,1)} %concatenate.73, bf16[8,8,5,1]{3,2,1,0:T(8,128)(2,1)} %copy.154, bf16[8,8,5,1]{3,2,1,0:T(8,128)(2,1)} %copy.155, bf16[8,8,5,110]{3,2,1,0:T(8,128)(2,1)S(1)} %broadcast_in_dim.9), dimensions={3} | concatenate | bytes 2293760 | tf_op jit(solution)/shard_map/concatenate | solution.py:141
  162.7 1.2 copy-done.4
  164.0 1.1 fusion.25
  165.1 2.0 convolution_convert_fusion
  167.2 53.7 %reduce-scatter.3.cloned.1.call-done = bf16[1,8,5,1792]{3,2,1,0:T(8,128)(2,1)} async-done(((bf16[8,8,5,1792]{3,2,1,0:T(8,128)(2,1)}), bf16[1,8,5,1792]{3,2,1,0:T(8,128)(2,1)}) %reduce-scatter.3.cloned.1.call-update) | async-done | bytes 143376 | tf_op jit(solution)/shard_map/reduce_scatter | solution.py:144
  220.9 29.1 %all_to_all.11 = bf16[8,5,1792]{2,1,0:T(8,128)(2,1)S(1)} all-to-all(bf16[8,5,1792]{2,1,0:T(8,128)(2,1)} %bitcast.103), channel_id=1, replica_groups={{0,64,128,192,256,320,384,448},{8,72,136,200,264,328,392,456},{16,80,14..., dimensions={0} | all-to-all | bytes 286720 | tf_op jit(solution)/shard_map/all_to_all | solution.py:147
  250.0 0.7 copy.156
  250.7 0.6 fusion.6
  251.3 1.4 fusion.32
  253.1 0.9 fusion.84
  253.9 18.8 %reduce-scatter.5.cloned.1.call-done = bf16[192,384]{1,0:T(8,128)(2,1)} async-done(((bf16[1536,384]{1,0:T(8,128)(2,1)}), bf16[192,384]{1,0:T(8,128)(2,1)}) %reduce-scatter.5.cloned.1.call-update) | async-done | bytes 147472 | tf_op jit(solution)/shard_map/reduce_scatter | solution.py:158
  272.7 1.7 convert_bitcast_fusion
  274.4 11.9 %all-gather.8.cloned.1.call-done = bf16[8,40,1792]{2,0,1:T(8,128)(2,1)} async-done(((bf16[8,5,1792]{2,0,1:T(8,128)(2,1)}), bf16[8,40,1792]{2,0,1:T(8,128)(2,1)}) %all-gather.8.cloned.1.call-update) | async-done | bytes 1146896 | tf_op jit(solution)/shard_map/all_gather | solution.py:150
  286.3 1.4 copy.157
  289.9 4.7 %collective-permute-start.2 = (f32[1,64,144]{1,2,0:T(8,128)S(1)}, f32[1,64,144]{1,2,0:T(8,128)S(1)}, u32[]{:S(2)}, u32[]{:S(2)}) collective-permute-start(f32[1,64,144]{1,2,0:T(8,128)S(1)} %get-tuple-element.45), channel_id=1, source_target_pairs={{0,8},{8,16},{16,24},{24,32},{32,40},{40,48},{48,56},{56,64},{64,7... | collective-permute-start | bytes 110600 | tf_op jit(solution)/shard_map/ppermute | solution.py:27
  294.6 1.9 collective-permute-start.3
  296.5 0.8 fusion.15
  297.5 4.6 %collective-permute-done.3 = f32[1,64,144]{1,2,0:T(8,128)S(1)} collective-permute-done((f32[1,64,144]{1,2,0:T(8,128)S(1)}, f32[1,64,144]{1,2,0:T(8,128)S(1)}, u32[]{:S(2)}, u32[]{:S(2)}) %collective-permute-start.3) | collective-permute-done | bytes 36896 | tf_op jit(solution)/shard_map/ppermute | solution.py:29
  302.0 0.5 select_maximum_fusion
  302.7 0.6 copy.163
  (121 shorter events, 8.6 us)
Async XLA Ops:
  8.0 16.5 %copy-start = (bf16[1536,8]{0,1:T(8,128)(2,1)S(1)}, bf16[1536,8]{0,1:T(8,128)(2,1)}, u32[]{:S(2)}) copy-start(bf16[1536,8]{0,1:T(8,128)(2,1)} %param.12) | copy-start | bytes 73732
  8.0 16.1 %copy-start.1 = (bf16[144,1536]{1,0:T(8,128)(2,1)S(1)}, bf16[144,1536]{1,0:T(8,128)(2,1)}, u32[]{:S(2)}) copy-start(bf16[144,1536]{1,0:T(8,128)(2,1)} %param.10) | copy-start | bytes 1327108
  8.0 16.5 %copy-start.17 = (f32[1536]{0:T(1024)S(1)}, f32[1536]{0:T(1024)}, u32[]{:S(2)}) copy-start(f32[1536]{0:T(1024)} %param.11) | copy-start | bytes 18436
  8.0 99.6 %all-gather.4.cloned.1.call-start = ((), (), s32[]{:S(2)}) async-start(), calls=%async_computation.4 | async-start | bytes 1290240 | tf_op jit(solution)/shard_map/all_gather | solution.py:117
  8.8 9.6 %collective-permute-start = (bf16[1,16,64]{2,1,0:T(8,128)(2,1)S(1)}, bf16[1,16,64]{2,1,0:T(8,128)(2,1)S(1)}, u32[]{:S(2)}, u32[]{:S(2)}) collective-permute-start(bf16[1,16,64]{2,1,0:T(8,128)(2,1)S(1)} %get-tuple-element.47), channel_id=1, source_target_pairs={{0,8},{8,16},{16,24},{24,32},{32,40},{40,48},{48,56},{56,64},{64,7... | collective-permute-start | bytes 6152 | tf_op jit(solution)/shard_map/ppermute | solution.py:27
  13.9 6.7 %collective-permute-start.1 = (bf16[1,16,64]{2,1,0:T(8,128)(2,1)S(1)}, bf16[1,16,64]{2,1,0:T(8,128)(2,1)S(1)}, u32[]{:S(2)}, u32[]{:S(2)}) collective-permute-start(bf16[1,16,64]{2,1,0:T(8,128)(2,1)S(1)} %get-tuple-element.48), channel_id=1, source_target_pairs={{8,0},{16,8},{24,16},{32,24},{40,32},{48,40},{56,48},{64,56},{72,6... | collective-permute-start | bytes 6152 | tf_op jit(solution)/shard_map/ppermute | solution.py:29
  16.8 8.0 %copy-start.16 = (s32[128,2]{0,1:T(2,128)S(1)}, s32[128,2]{0,1:T(2,128)}, u32[]{:S(2)}) copy-start(s32[128,2]{0,1:T(2,128)} %param.13) | copy-start | bytes 3076
  21.4 4.2 %copy-start.6 = (bf16[128,1536]{1,0:T(8,128)(2,1)S(1)}, bf16[128,1536]{1,0:T(8,128)(2,1)}, u32[]{:S(2)}) copy-start(bf16[128,1536]{1,0:T(8,128)(2,1)} %param.17) | copy-start | bytes 1179652
  25.7 33.1 %copy-start.14 = (bf16[192,384]{1,0:T(8,128)(2,1)S(1)}, bf16[192,384]{1,0:T(8,128)(2,1)}, u32[]{:S(2)}) copy-start(bf16[192,384]{1,0:T(8,128)(2,1)} %param.14) | copy-start | bytes 442372
  25.7 33.1 %copy-start.15 = (bf16[192,384]{1,0:T(8,128)(2,1)S(1)}, bf16[192,384]{1,0:T(8,128)(2,1)}, u32[]{:S(2)}) copy-start(bf16[192,384]{1,0:T(8,128)(2,1)} %param.15) | copy-start | bytes 442372
  58.6 76.8 %all-reduce.5.cloned.1.call-start = ((), (), s32[]{:S(2)}) async-start(), calls=%async_computation.5 | async-start | bytes 884736 | tf_op jit(solution)/shard_map/psum | solution.py:68
  60.2 89.4 %all-gather.6.cloned.1.call-start = ((), (), s32[]{:S(2)}) async-start(), calls=%async_computation.6 | async-start | bytes 1327104 | tf_op jit(solution)/shard_map/all_gather | solution.py:70
  61.0 159.9 %reduce-scatter.3.cloned.1.call-start = ((), (), s32[]{:S(2)}) async-start(), calls=%async_computation.7 | async-start | bytes 2064384 | tf_op jit(solution)/shard_map/reduce_scatter | solution.py:144
  111.9 25.0 %copy-start.3 = (bf16[320,1792]{1,0:T(8,128)(2,1)S(1)}, bf16[320,1792]{1,0:T(8,128)(2,1)}, u32[]{:S(2)}) copy-start(bf16[320,1792]{1,0:T(8,128)(2,1)} %reshape.240) | copy-start | bytes 3440644
  135.4 1.4 copy-start.2
  152.7 2.9 copy-start.8
  152.7 3.0 copy-start.10
  155.3 1.3 copy-start.12
  162.6 1.3 copy-start.4
  162.6 1.3 copy-start.9
  162.6 1.4 copy-start.11
  162.6 2.5 copy-start.13
  162.7 88.6 %all-reduce.7.cloned.1.call-start = ((), (), s32[]{:S(2)}) async-start(), calls=%async_computation.9 | async-start | bytes 884736 | tf_op jit(solution)/shard_map/psum | solution.py:151
  165.1 107.6 %reduce-scatter.5.cloned.1.call-start = ((), (), s32[]{:S(2)}) async-start(), calls=%async_computation.10 | async-start | bytes 1327104 | tf_op jit(solution)/shard_map/reduce_scatter | solution.py:158
  167.2 119.1 %all-gather.8.cloned.1.call-start = ((), (), s32[]{:S(2)}) async-start(), calls=%async_computation.8 | async-start | bytes 1290240 | tf_op jit(solution)/shard_map/all_gather | solution.py:150
  251.3 1.4 copy-start.5
  288.2 1.0 copy-start.7
  289.9 7.6 %collective-permute-start.2 = (f32[1,64,144]{1,2,0:T(8,128)S(1)}, f32[1,64,144]{1,2,0:T(8,128)S(1)}, u32[]{:S(2)}, u32[]{:S(2)}) collective-permute-start(f32[1,64,144]{1,2,0:T(8,128)S(1)} %get-tuple-element.45), channel_id=1, source_target_pairs={{0,8},{8,16},{16,24},{24,32},{32,40},{40,48},{48,56},{56,64},{64,7... | collective-permute-start | bytes 110600 | tf_op jit(solution)/shard_map/ppermute | solution.py:27
  294.6 7.5 %collective-permute-start.3 = (f32[1,64,144]{1,2,0:T(8,128)S(1)}, f32[1,64,144]{1,2,0:T(8,128)S(1)}, u32[]{:S(2)}, u32[]{:S(2)}) collective-permute-start(f32[1,64,144]{1,2,0:T(8,128)S(1)} %get-tuple-element.46), channel_id=1, source_target_pairs={{8,0},{16,8},{24,16},{32,24},{40,32},{48,40},{56,48},{64,56},{72,6... | collective-permute-start | bytes 110600 | tf_op jit(solution)/shard_map/ppermute | solution.py:29
Sparse Core Ops, SparseCore 0:
  58.7 48.8 all-gather.3
  109.8 39.7 all-gather.5
  162.8 58.0 reduce-scatter.2
  223.6 49.1 reduce-scatter.4
Sparse Core Ops, SparseCore 1:
  61.5 73.9 all-reduce.4
  165.5 77.1 all-reduce.6
  250.8 35.4 all-gather.7
where the time goes:
time: 312 us; the launch traced here: 311 us
  waiting for transfers between devices  173 us (55%)
  blocking collectives  60.9 us (20%)
  local copies, waits for them, and re-layouts  19.4 us (6%)
  matrix products  18.2 us (6%)
  between operations  16 us (5%)
  starting transfers between devices  13.8 us (4%)
  other arithmetic  9.23 us (3%)
    reduce_scatter x1, waiting for transfers between devices, local(): lax.psum_scatter(ret, 'exp', scatter_dimension=0, axis_index_groups=along...  53.7 us
    all_gather x1, waiting for transfers between devices, local(): lax.all_gather(stage, 'exp', axis=0, tiled=True, axis_index_groups=along)  46.7 us
    all_to_all x1, blocking collectives, local(): lax.all_to_all(send, 'exp', split_axis=0, concat_axis=0, tiled=True, axis...  31.8 us
    all_to_all x1, blocking collectives, local(): lax.all_to_all(summed, 'exp', split_axis=0, concat_axis=0, tiled=True, ax...  29.1 us
    psum x1, waiting for transfers between devices, local(): g_full = lax.psum(dot32(sg_hi, w2) + dot32(sg_lo, w2), 'rep')  23.1 us
    reduce_scatter x1, waiting for transfers between devices, local(): lax.psum_scatter(d_part.astype(BF), 'rep', scatter_dimension=0, tiled=True)  18.8 us
    all_gather x1, waiting for transfers between devices, local(): lax.all_gather(mine, 'rep', axis=1, tiled=True).reshape(experts * CAP, -1)  11.9 us
    all_gather x1, waiting for transfers between devices, local(): down = lax.all_gather(down_weight, 'rep', axis=1, tiled=True)  11.5 us
  transfers between devices with their start and end apart: 11, of which 8 were waited for; matrix products, arithmetic and copies ran while one was open for 7% of the time, Pallas kernels for 0%

commit v1 on v0

--- a/solution.py
+++ b/solution.py
@@ -65,7 +65,9 @@
     gain_here = lax.dynamic_slice_in_dim(norm_gain, rep * dsl, dsl, 0)
     sg_hi, sg_lo = split(s_here.astype(F32) * gain_here)
     w2 = jnp.concatenate([gate_weight, up_weight], axis=1)
-    g_full = lax.psum(dot32(sg_hi, w2) + dot32(sg_lo, w2), "rep")
+    own = dot32(sg_hi, w2) + dot32(sg_lo, w2)
+    blocks = lax.all_gather(own, "rep")
+    g_full = jnp.sum(blocks, axis=0)
     g_hi, g_lo = split(g_full)
     down = lax.all_gather(down_weight, "rep", axis=1, tiled=True)
     padded = jnp.pad(halo(latent), ((0, 0), (0, 0), (1, 1)))

time: 312 us -> 444 us (1.42)
  waiting for transfers between devices: 173 us -> 310 us
    psum x1, waiting for transfers between devices: 0.03 us -> 57.5 us  [local(): t_full = lax.psum(t_part, 'rep')]
    all_gather x0 -> x1, waiting for transfers between devices: none -> 44.2 us  [local(): blocks = lax.all_gather(own, 'rep')]
    psum x1 -> x0, waiting for transfers between devices: 23.1 us -> none  [local(): g_full = lax.psum(dot32(sg_hi, w2) + dot32(sg_lo, w2), 'rep')]
    reduce_scatter x1, waiting for transfers between devices: 18.8 us -> 39.1 us  [local(): lax.psum_scatter(d_part.astype(BF), 'rep', scatter_dimension=0, tiled=True)]
    all_gather x1, waiting for transfers between devices: 11.5 us -> 30.4 us  [local(): down = lax.all_gather(down_weight, 'rep', axis=1, tiled=True)]
    all_gather x1, waiting for transfers between devices: 11.9 us -> 30.5 us  [local(): lax.all_gather(mine, 'rep', axis=1, tiled=True).reshape(experts * CAP, -1)]
  transfers between devices with their start and end apart: 11 -> 11, of which waited for: 8 -> 9; matrix products, arithmetic and copies ran while one was open for 7% -> 4% of each run, Pallas kernels for 0% -> 0%
where the time goes in v1:
time: 444 us
  waiting for transfers between devices  310 us (70%)
  blocking collectives  60.4 us (14%)
  local copies, waits for them, and re-layouts  17 us (4%)
  matrix products  16.4 us (4%)
  between operations  14.8 us (3%)
  starting transfers between devices  13.8 us (3%)
  other arithmetic  11.1 us (2%)
    psum x1, waiting for transfers between devices, local(): t_full = lax.psum(t_part, 'rep')  57.5 us
    reduce_scatter x1, waiting for transfers between devices, local(): lax.psum_scatter(ret, 'exp', scatter_dimension=0, axis_index_groups=along...  53.9 us
    all_gather x1, waiting for transfers between devices, local(): lax.all_gather(stage, 'exp', axis=0, tiled=True, axis_index_groups=along)  46.8 us
    all_gather x1, waiting for transfers between devices, local(): blocks = lax.all_gather(own, 'rep')  44.2 us
    reduce_scatter x1, waiting for transfers between devices, local(): lax.psum_scatter(d_part.astype(BF), 'rep', scatter_dimension=0, tiled=True)  39.1 us
    all_to_all x1, blocking collectives, local(): lax.all_to_all(send, 'exp', split_axis=0, concat_axis=0, tiled=True, axis...  31.8 us
    all_gather x1, waiting for transfers between devices, local(): lax.all_gather(mine, 'rep', axis=1, tiled=True).reshape(experts * CAP, -1)  30.5 us
    all_gather x1, waiting for transfers between devices, local(): down = lax.all_gather(down_weight, 'rep', axis=1, tiled=True)  30.4 us
  transfers between devices with their start and end apart: 11, of which 9 were waited for; matrix products, arithmetic and copies ran while one was open for 4% of the time, Pallas kernels for 0%

profile of v1, /device:TPU:96, one launch (start us, length us, event | category | flops | bytes accessed | tf_op | source)
XLA Modules:
  0.0 443.5 jit_solution(16337189508034964792)
XLA Ops:
  7.2 0.8 fusion.85
  8.0 5.0 %collective-permute-start = (bf16[1,16,64]{2,1,0:T(8,128)(2,1)S(1)}, bf16[1,16,64]{2,1,0:T(8,128)(2,1)S(1)}, u32[]{:S(2)}, u32[]{:S(2)}) collective-permute-start(bf16[1,16,64]{2,1,0:T(8,128)(2,1)S(1)} %get-tuple-element.47), channel_id=1, source_target_pairs={{0,8},{8,16},{16,24},{24,32},{32,40},{40,48},{48,56},{56,64},{64,7... | collective-permute-start | bytes 6152 | tf_op jit(solution)/shard_map/ppermute | solution.py:27
  13.0 1.9 collective-permute-start.1
  15.0 0.7 convert_reduce_fusion
  16.0 0.7 multiply_reduce_fusion.3
  16.7 0.7 multiply_add_fusion.1
  17.7 2.1 collective-permute-done.1
  19.7 0.8 fusion.59
  20.5 0.8 constant_dynamic-update-slice_fusion.7
  21.4 0.7 constant_dynamic-update-slice_fusion.4
  22.2 0.7 constant_dynamic-update-slice_fusion.1
  23.6 0.6 copy-done.27
  26.0 31.8 %all_to_all.10 = bf16[8,5,1792]{2,1,0:T(8,128)(2,1)S(1)} all-to-all(bf16[8,5,1792]{2,1,0:T(8,128)(2,1)S(1)} %reshape.239), channel_id=1, replica_groups={{0,64,128,192,256,320,384,448},{8,72,136,200,264,328,392,456},{16,80,14..., dimensions={0} | all-to-all | bytes 286720 | tf_op jit(solution)/shard_map/all_to_all | solution.py:116
  57.7 0.7 copy.149
  58.9 1.1 convolution_add_fusion.2
  60.0 0.7 all-gather.8.cloned.1.call-update
  60.8 46.8 %all-gather.6.cloned.1.call-done = bf16[64,5,1792]{2,0,1:T(8,128)(2,1)} async-done(((bf16[8,5,1792]{2,0,1:T(8,128)(2,1)}), bf16[64,5,1792]{2,0,1:T(8,128)(2,1)}) %all-gather.6.cloned.1.call-update) | async-done | bytes 1146896 | tf_op jit(solution)/shard_map/all_gather | solution.py:119
  107.6 1.9 copy.150
  109.5 0.5 reshape.240
  110.2 0.9 multiply_reduce_fusion.1
  111.0 44.2 %all-gather.12.cloned.1.call-done = f32[1152,768]{1,0:T(8,128)} async-done(((f32[144,768]{1,0:T(8,128)}), f32[1152,768]{1,0:T(8,128)}) %all-gather.12.cloned.1.call-update) | async-done | bytes 3538960 | tf_op jit(solution)/shard_map/all_gather | solution.py:69
  155.3 2.3 reduce_sum.123
  158.1 30.4 %all-gather.8.cloned.1.call-done = bf16[384,1536]{0,1:T(8,128)(2,1)} async-done(((bf16[384,192]{0,1:T(8,128)(2,1)}), bf16[384,1536]{0,1:T(8,128)(2,1)}) %all-gather.8.cloned.1.call-update) | async-done | bytes 1179664 | tf_op jit(solution)/shard_map/all_gather | solution.py:72
  188.5 3.5 multiply_convert_fusion.1
  193.4 2.0 convolution_convert_fusion.1
  195.8 0.8 reduce_sum.125
  197.5 2.1 concatenate.74
  199.7 1.2 copy-done.5
  200.9 1.1 fusion.25
  202.0 2.0 convolution_convert_fusion
  204.1 53.9 %reduce-scatter.3.cloned.1.call-done = bf16[1,8,5,1792]{3,2,1,0:T(8,128)(2,1)} async-done(((bf16[8,8,5,1792]{3,2,1,0:T(8,128)(2,1)}), bf16[1,8,5,1792]{3,2,1,0:T(8,128)(2,1)}) %reduce-scatter.3.cloned.1.call-update) | async-done | bytes 143376 | tf_op jit(solution)/shard_map/reduce_scatter | solution.py:146
  258.1 28.7 %all_to_all.11 = bf16[8,5,1792]{2,1,0:T(8,128)(2,1)S(1)} all-to-all(bf16[8,5,1792]{2,1,0:T(8,128)(2,1)} %bitcast.105), channel_id=1, replica_groups={{0,64,128,192,256,320,384,448},{8,72,136,200,264,328,392,456},{16,80,14..., dimensions={0} | all-to-all | bytes 286720 | tf_op jit(solution)/shard_map/all_to_all | solution.py:149
  286.7 0.7 copy.156
  287.4 0.6 fusion.6
  288.0 57.5 %all-reduce.4.cloned.1.call-done = f32[144,768]{1,0:T(8,128)} async-done(((f32[144,768]{1,0:T(8,128)}), f32[144,768]{1,0:T(8,128)}) %all-reduce.4.cloned.1.call-update) | async-done | bytes 442384 | tf_op jit(solution)/shard_map/psum | solution.py:153
  345.5 1.4 fusion.32
  347.3 0.9 fusion.84
  348.2 39.1 %reduce-scatter.5.cloned.1.call-done = bf16[192,384]{1,0:T(8,128)(2,1)} async-done(((bf16[1536,384]{1,0:T(8,128)(2,1)}), bf16[192,384]{1,0:T(8,128)(2,1)}) %reduce-scatter.5.cloned.1.call-update) | async-done | bytes 147472 | tf_op jit(solution)/shard_map/reduce_scatter | solution.py:160
  387.2 1.6 convert_bitcast_fusion
  388.9 30.5 %all-gather.10.cloned.1.call-done = bf16[8,40,1792]{2,0,1:T(8,128)(2,1)} async-done(((bf16[8,5,1792]{2,0,1:T(8,128)(2,1)}), bf16[8,40,1792]{2,0,1:T(8,128)(2,1)}) %all-gather.10.cloned.1.call-update) | async-done | bytes 1146896 | tf_op jit(solution)/shard_map/all_gather | solution.py:152
  419.4 1.4 copy.157
  421.4 0.4 fusion.37
  423.3 4.7 %collective-permute-start.2 = (f32[1,64,144]{1,2,0:T(8,128)S(1)}, f32[1,64,144]{1,2,0:T(8,128)S(1)}, u32[]{:S(2)}, u32[]{:S(2)}) collective-permute-start(f32[1,64,144]{1,2,0:T(8,128)S(1)} %get-tuple-element.45), channel_id=1, source_target_pairs={{0,8},{8,16},{16,24},{24,32},{32,40},{40,48},{48,56},{56,64},{64,7... | collective-permute-start | bytes 110600 | tf_op jit(solution)/shard_map/ppermute | solution.py:27
  427.9 1.9 collective-permute-start.3
  429.9 0.8 fusion.15
  430.8 4.6 %collective-permute-done.3 = f32[1,64,144]{1,2,0:T(8,128)S(1)} collective-permute-done((f32[1,64,144]{1,2,0:T(8,128)S(1)}, f32[1,64,144]{1,2,0:T(8,128)S(1)}, u32[]{:S(2)}, u32[]{:S(2)}) %collective-permute-start.3) | collective-permute-done | bytes 36896 | tf_op jit(solution)/shard_map/ppermute | solution.py:29
  435.4 0.5 select_maximum_fusion
  436.1 0.6 copy.163
  (144 shorter events, 9.6 us)
Async XLA Ops:
  7.2 17.0 %copy-start = (bf16[1536,8]{0,1:T(8,128)(2,1)S(1)}, bf16[1536,8]{0,1:T(8,128)(2,1)}, u32[]{:S(2)}) copy-start(bf16[1536,8]{0,1:T(8,128)(2,1)} %param.12) | copy-start | bytes 73732
  7.2 16.0 %copy-start.1 = (bf16[144,1536]{1,0:T(8,128)(2,1)S(1)}, bf16[144,1536]{1,0:T(8,128)(2,1)}, u32[]{:S(2)}) copy-start(bf16[144,1536]{1,0:T(8,128)(2,1)} %param.10) | copy-start | bytes 1327108
  7.2 17.0 %copy-start.18 = (f32[1536]{0:T(1024)S(1)}, f32[1536]{0:T(1024)}, u32[]{:S(2)}) copy-start(f32[1536]{0:T(1024)} %param.11) | copy-start | bytes 18436
  7.2 100.4 %all-gather.6.cloned.1.call-start = ((), (), s32[]{:S(2)}) async-start(), calls=%async_computation.4 | async-start | bytes 1290240 | tf_op jit(solution)/shard_map/all_gather | solution.py:119
  8.0 9.7 %collective-permute-start = (bf16[1,16,64]{2,1,0:T(8,128)(2,1)S(1)}, bf16[1,16,64]{2,1,0:T(8,128)(2,1)S(1)}, u32[]{:S(2)}, u32[]{:S(2)}) collective-permute-start(bf16[1,16,64]{2,1,0:T(8,128)(2,1)S(1)} %get-tuple-element.47), channel_id=1, source_target_pairs={{0,8},{8,16},{16,24},{24,32},{32,40},{40,48},{48,56},{56,64},{64,7... | collective-permute-start | bytes 6152 | tf_op jit(solution)/shard_map/ppermute | solution.py:27
  13.0 6.7 %collective-permute-start.1 = (bf16[1,16,64]{2,1,0:T(8,128)(2,1)S(1)}, bf16[1,16,64]{2,1,0:T(8,128)(2,1)S(1)}, u32[]{:S(2)}, u32[]{:S(2)}) collective-permute-start(bf16[1,16,64]{2,1,0:T(8,128)(2,1)S(1)} %get-tuple-element.48), channel_id=1, source_target_pairs={{8,0},{16,8},{24,16},{32,24},{40,32},{48,40},{56,48},{64,56},{72,6... | collective-permute-start | bytes 6152 | tf_op jit(solution)/shard_map/ppermute | solution.py:29
  16.0 8.5 %copy-start.17 = (s32[128,2]{0,1:T(2,128)S(1)}, s32[128,2]{0,1:T(2,128)}, u32[]{:S(2)}) copy-start(s32[128,2]{0,1:T(2,128)} %param.13) | copy-start | bytes 3076
  17.4 3.1 copy-start.21
  17.4 7.1 %copy-start.19 = (s32[128]{0:T(128)}, s32[128]{0:T(128)S(1)}, u32[]{:S(2)}) copy-start(s32[128]{0:T(128)S(1)} %get-tuple-element.55) | copy-start | bytes 1540
  20.5 4.8 %copy-start.7 = (bf16[128,1536]{1,0:T(8,128)(2,1)S(1)}, bf16[128,1536]{1,0:T(8,128)(2,1)}, u32[]{:S(2)}) copy-start(bf16[128,1536]{1,0:T(8,128)(2,1)} %param.17) | copy-start | bytes 1179652
  23.1 2.2 copy-start.11
  23.5 1.8 copy-start.25
  23.6 2.2 copy-start.2
  23.6 0.6 copy-start.27
  24.5 0.8 copy-start.23
  25.5 33.1 %copy-start.15 = (bf16[192,384]{1,0:T(8,128)(2,1)S(1)}, bf16[192,384]{1,0:T(8,128)(2,1)}, u32[]{:S(2)}) copy-start(bf16[192,384]{1,0:T(8,128)(2,1)} %param.14) | copy-start | bytes 442372
  25.5 33.1 %copy-start.16 = (bf16[192,384]{1,0:T(8,128)(2,1)S(1)}, bf16[192,384]{1,0:T(8,128)(2,1)}, u32[]{:S(2)}) copy-start(bf16[192,384]{1,0:T(8,128)(2,1)} %param.15) | copy-start | bytes 442372
  58.4 96.8 %all-gather.12.cloned.1.call-start = ((), (), s32[]{:S(2)}) async-start(), calls=%async_computation.10 | async-start | bytes 3981312 | tf_op jit(solution)/shard_map/all_gather | solution.py:69
  60.0 128.5 %all-gather.8.cloned.1.call-start = ((), (), s32[]{:S(2)}) async-start(), calls=%async_computation.5 | async-start | bytes 1327104 | tf_op jit(solution)/shard_map/all_gather | solution.py:72
  60.7 197.3 %reduce-scatter.3.cloned.1.call-start = ((), (), s32[]{:S(2)}) async-start(), calls=%async_computation.6 | async-start | bytes 2064384 | tf_op jit(solution)/shard_map/reduce_scatter | solution.py:146
  110.1 78.5 %copy-start.4 = (bf16[320,1792]{1,0:T(8,128)(2,1)}, bf16[320,1792]{1,0:T(8,128)(2,1)S(1)}, u32[]{:S(2)}) copy-start(bf16[320,1792]{1,0:T(8,128)(2,1)S(1)} %reshape.240) | copy-start | bytes 3440644
  192.0 0.7 copy-start.9
  192.4 1.0 copy-start.13
  199.6 1.3 copy-start.5
  199.6 1.3 copy-start.10
  199.6 2.4 copy-start.14
  199.6 145.9 %all-reduce.4.cloned.1.call-start = ((), (), s32[]{:S(2)}) async-start(), calls=%async_computation.8 | async-start | bytes 884736 | tf_op jit(solution)/shard_map/psum | solution.py:153
  202.0 185.3 %reduce-scatter.5.cloned.1.call-start = ((), (), s32[]{:S(2)}) async-start(), calls=%async_computation.9 | async-start | bytes 1327104 | tf_op jit(solution)/shard_map/reduce_scatter | solution.py:160
  204.0 83.9 %copy-start.24 = (f32[128]{0:T(128)S(1)}, f32[128]{0:T(128)}, u32[]{:S(2)}) copy-start(f32[128]{0:T(128)} %copy-done.23) | copy-start | bytes 1540
  204.1 215.3 %all-gather.10.cloned.1.call-start = ((), (), s32[]{:S(2)}) async-start(), calls=%async_computation.7 | async-start | bytes 1290240 | tf_op jit(solution)/shard_map/all_gather | solution.py:152
  345.5 1.4 copy-start.6
  388.9 32.0 %copy-start.20 = (s32[128]{0:T(128)S(1)}, s32[128]{0:T(128)}, u32[]{:S(2)}) copy-start(s32[128]{0:T(128)} %copy-done.19) | copy-start | bytes 1540
  388.9 32.2 %copy-start.22 = (s32[128]{0:T(128)S(1)}, s32[128]{0:T(128)}, u32[]{:S(2)}) copy-start(s32[128]{0:T(128)} %copy-done.21) | copy-start | bytes 1540
  421.4 0.8 copy-start.12
  421.4 0.8 copy-start.28
  421.4 1.1 copy-start.26
  421.4 1.1 copy-start.8
  421.9 1.0 copy-start.3
  423.3 7.6 %collective-permute-start.2 = (f32[1,64,144]{1,2,0:T(8,128)S(1)}, f32[1,64,144]{1,2,0:T(8,128)S(1)}, u32[]{:S(2)}, u32[]{:S(2)}) collective-permute-start(f32[1,64,144]{1,2,0:T(8,128)S(1)} %get-tuple-element.45), channel_id=1, source_target_pairs={{0,8},{8,16},{16,24},{24,32},{32,40},{40,48},{48,56},{56,64},{64,7... | collective-permute-start | bytes 110600 | tf_op jit(solution)/shard_map/ppermute | solution.py:27
  427.9 7.5 %collective-permute-start.3 = (f32[1,64,144]{1,2,0:T(8,128)S(1)}, f32[1,64,144]{1,2,0:T(8,128)S(1)}, u32[]{:S(2)}, u32[]{:S(2)}) collective-permute-start(f32[1,64,144]{1,2,0:T(8,128)S(1)} %get-tuple-element.46), channel_id=1, source_target_pairs={{8,0},{16,8},{24,16},{32,24},{40,32},{48,40},{56,48},{64,56},{72,6... | collective-permute-start | bytes 110600 | tf_op jit(solution)/shard_map/ppermute | solution.py:29
Sparse Core Ops, SparseCore 0:
  58.6 49.0 all-gather.5
  109.7 45.4 all-gather.11
  157.4 31.1 all-gather.7
  199.7 58.2 reduce-scatter.2
  260.2 85.2 all-reduce.3
  348.2 38.9 reduce-scatter.4
  389.4 29.9 all-gather.9
